TPU v7x, 32 devices: a whole 2x2x4 slice. The times are simulated.
32 devices in a mesh: seg: 4 (over y, core), ep: 8 (over z, x).
Axes of the slice: x: 2, y: 2, z: 4, core: 2. Of those that a mesh axis runs over, the one named last changes fastest.
Arguments:
- queries: bfloat16 [2048, 2048], P(('seg', 'ep')), may hold values from -6 to 6
- keys: bfloat16 [2048, 2048], P(('seg', 'ep')), may hold values from -1.25 to 1.25
- values: bfloat16 [2048, 2048], P(('seg', 'ep')), may hold values from -54 to 54
- log_decay: float32 [2048, 16], P('seg', 'ep'), may hold values from -1 to 0
- out_gain: float32 [2048], replicated, may hold values from 0.1 to 1.9
- out_proj: bfloat16 [2048, 6144], P('ep', 'seg'), may hold values from -0.125 to 0.125
- experts: int32 [256, 2], P(('seg', 'ep')), may hold values from 0 to 3, all different within a row; in each aligned block of 8 rows (0 to 7, 8 to 15, ...) at most 8 rows name the same one
- gates: float32 [256, 2], P(('seg', 'ep')), may hold values from 0.2 to 1
- up_weight: bfloat16 [8, 6144, 2304], P('ep', None, 'seg'), may hold values from -0.078125 to 0.078125
- down_weight: bfloat16 [8, 2304, 6144], P('ep', 'seg'), may hold values from -0.09375 to 0.09375
Outputs:
- attn_out: bfloat16 [2048, 2048], P(('seg', 'ep'))
- moe_out: bfloat16 [256, 6144], P(('seg', 'ep'))
Inputs may be any that keep to these rules, and one draw needn't show every extreme that they name: Each row names two different experts. The 8 rows of one device name any one expert at most 8 times, and in some devices one expert exactly 8 times.
All inputs are finite; a program needn't handle non-finite values.
Results may differ from a plain program's by a relative error of at most 0.025.
Values may be sent and summed in bfloat16 or wider, within the bound.
A program may use at most 128 MiB of HBM per device.

v0:
```python
import math

import jax
import jax.numpy as jnp
from jax import lax
from jax.sharding import PartitionSpec as P

epsilon = 1e-06


def prefix(x, axis, join, neutral):
    place = lax.axis_index(axis)
    gathered = jax.tree.map(
        lambda a, kind: lax.all_gather(a.astype(kind), axis), x, (jnp.bfloat16, jnp.bfloat16)
    )
    state = jax.tree.map(lambda a, e: jnp.zeros_like(a) + jnp.asarray(e, a.dtype), x, neutral)

    def one(turn, state):
        return join(
            state,
            jax.tree.map(
                lambda a, own: lax.dynamic_index_in_dim(a, turn, 0, False).astype(own.dtype),
                gathered,
                x,
            ),
        )

    return lax.fori_loop(0, place, one, state)


def chain_combine(first_part, second_part):
    return (
        first_part[0] * second_part[0],
        second_part[0][:, None, None] * first_part[1] + second_part[1],
    )


def route_tables(experts, gates, expert_count, capacity):
    token_count = experts.shape[0]
    flattened = experts.reshape(-1)
    onehot = (flattened[:, None] == jnp.arange(expert_count, dtype=jnp.int32)[None, :]).astype(
        jnp.int32
    )
    earlier = jnp.cumsum(onehot, axis=0) - onehot
    position = jnp.sum(earlier * onehot, axis=1)
    slot_index = (flattened * capacity + position).reshape(token_count, 2)
    columns = jnp.arange(expert_count * capacity, dtype=jnp.int32)
    matches = slot_index[:, :, None] == columns[None, None, :]
    dispatch = jnp.any(matches, axis=1).T.astype(jnp.bfloat16)
    combine = jnp.sum(jnp.where(matches, gates[:, :, None], 0.0), axis=1)
    return (dispatch, combine)


def expert_output(row_data, up_piece, down_piece):
    hidden = jax.nn.silu(jnp.dot(row_data, up_piece, preferred_element_type=jnp.float32)).astype(
        jnp.bfloat16
    )
    return jnp.dot(hidden, down_piece, preferred_element_type=jnp.float32)


def on_device(
    queries, keys, values, log_decay, out_gain, out_proj, experts, gates, up_weight, down_weight
):
    highest = lax.Precision.HIGHEST
    ep_count = lax.axis_size("ep")
    heads_local = log_decay.shape[1]
    head_dim = queries.shape[1] // (heads_local * ep_count)
    query_heads, key_heads, value_heads = (
        lax.all_to_all(queries, "ep", split_axis=1, concat_axis=0, tiled=True),
        lax.all_to_all(keys, "ep", split_axis=1, concat_axis=0, tiled=True),
        lax.all_to_all(values, "ep", split_axis=1, concat_axis=0, tiled=True),
    )
    seg_length = query_heads.shape[0]
    query_heads = query_heads.reshape(seg_length, heads_local, head_dim)
    key_heads = key_heads.reshape(seg_length, heads_local, head_dim)
    value_heads = value_heads.reshape(seg_length, heads_local, head_dim)
    cumulative = jnp.cumsum(log_decay, axis=0)
    across = cumulative.T
    block_size = math.gcd(seg_length, 512)
    starts = jnp.arange(seg_length // block_size, dtype=jnp.int32) * block_size
    token_positions = jnp.arange(seg_length, dtype=jnp.int32)

    def block_mix(start):
        query_block = lax.dynamic_slice_in_dim(query_heads, start, block_size, 0)
        cum_block = lax.dynamic_slice_in_dim(across, start, block_size, 1)
        row_ids = start + jnp.arange(block_size, dtype=jnp.int32)
        causal = (row_ids[:, None] >= token_positions[None, :])[None]
        log_gap = cum_block[:, :, None] - across[:, None, :]
        weight = jnp.where(causal, jnp.exp(jnp.where(causal, log_gap, 0.0)), 0.0)
        scores = jnp.einsum(
            "thd,shd->hts", query_block, key_heads, preferred_element_type=jnp.float32
        )
        mixing = (scores * weight).astype(jnp.bfloat16)
        return jnp.einsum("hts,she->the", mixing, value_heads, preferred_element_type=jnp.float32)

    inside = lax.map(block_mix, starts).reshape(seg_length, heads_local, head_dim)
    ending = cumulative[-1]
    to_end = jnp.exp(ending[None, :] - cumulative)
    key_float = key_heads.astype(jnp.float32)
    value_float = value_heads.astype(jnp.float32)
    local_state = jnp.einsum("sh,shd,she->hde", to_end, key_float, value_float, precision=highest)
    identity = (jnp.ones_like(ending), jnp.zeros_like(local_state))
    carried = prefix((jnp.exp(ending), local_state), "seg", chain_combine, identity)[1]
    outside = jnp.exp(cumulative)[:, :, None] * jnp.einsum(
        "thd,hde->the", query_heads.astype(jnp.float32), carried, precision=highest
    )
    mixture = (inside + outside).astype(jnp.bfloat16).reshape(seg_length, heads_local * head_dim)
    token_mix = lax.all_to_all(mixture, "ep", split_axis=0, concat_axis=1, tiled=True)
    as_float = token_mix.astype(jnp.float32)
    inv_rms = lax.rsqrt(jnp.mean(as_float * as_float, axis=1, keepdims=True) + epsilon)
    attn_out = (as_float * inv_rms * out_gain[None, :]).astype(jnp.bfloat16)
    row_stride = 8
    own_width = heads_local * head_dim
    feature_count = own_width * ep_count
    picked_float = mixture.reshape(seg_length // row_stride, row_stride, own_width)[:, 0].astype(
        jnp.float32
    )
    square_sums = lax.psum(jnp.sum(picked_float * picked_float, axis=1), "ep")
    picked_rms = lax.rsqrt(square_sums[:, None] / feature_count + epsilon)
    gain_slice = lax.dynamic_slice_in_dim(out_gain, lax.axis_index("ep") * own_width, own_width, 0)
    normed_rows = (picked_float * picked_rms * gain_slice[None, :]).astype(jnp.bfloat16)
    proj_terms = jnp.dot(
        normed_rows,
        lax.all_gather(out_proj, "seg", axis=1, tiled=True),
        preferred_element_type=jnp.float32,
    )
    moe_in = lax.psum_scatter(
        proj_terms.astype(jnp.bfloat16), "ep", scatter_dimension=0, tiled=True
    )
    expert_count = ep_count // 2
    token_count, model_width = moe_in.shape
    capacity = max(2, 4 * token_count // expert_count)
    dispatch, combine = route_tables(experts, gates, expert_count, capacity)
    up_piece = up_weight[0]
    down_piece = down_weight[0]
    slot_rows = jnp.dot(dispatch, moe_in, preferred_element_type=jnp.float32).astype(jnp.bfloat16)
    outgoing = jnp.repeat(slot_rows.reshape(expert_count, capacity, model_width), 2, axis=0)
    arrived = lax.all_to_all(outgoing, "ep", split_axis=0, concat_axis=0, tiled=True).reshape(
        ep_count * capacity, model_width
    )
    gathered = lax.all_gather(arrived, "seg", axis=0, tiled=True)
    owned_sums = lax.psum_scatter(
        expert_output(gathered, up_piece, down_piece).astype(jnp.bfloat16),
        "seg",
        scatter_dimension=0,
        tiled=True,
    ).astype(jnp.float32)
    returned_back = lax.all_to_all(
        owned_sums.reshape(ep_count, capacity, model_width).astype(jnp.bfloat16),
        "ep",
        split_axis=0,
        concat_axis=0,
        tiled=True,
    ).astype(jnp.float32)
    paired = returned_back.reshape(expert_count, 2, capacity, model_width)
    halves = (paired[:, 0] + paired[:, 1]).reshape(expert_count * capacity, model_width)
    summed = jnp.dot(combine, halves, precision=highest)
    moe_out = summed.astype(jnp.bfloat16)
    return (attn_out, moe_out)


def solution(mesh):
    placed = (
        P(("seg", "ep"), None),
        P(("seg", "ep"), None),
        P(("seg", "ep"), None),
        P("seg", "ep"),
        P(),
        P("ep", "seg"),
        P(("seg", "ep"), None),
        P(("seg", "ep"), None),
        P("ep", None, "seg"),
        P("ep", "seg", None),
    )
    return jax.shard_map(
        on_device,
        mesh=mesh,
        in_specs=placed,
        out_specs=(P(("seg", "ep"), None), P(("seg", "ep"), None)),
        check_vma=False,
    )
```

profile of v0, /device:TPU:0, one launch (start us, length us, event | category | flops | bytes accessed | tf_op | source)
XLA Modules:
  0.0 282.9 jit_solution(439262611105810195)
XLA Ops:
  7.2 1.7 copy.181
  8.8 7.3 %all-to-all-start.1 = ((bf16[64,8,256]{2,0,1:T(8,128)(2,1)}), bf16[64,8,256]{2,0,1:T(8,128)(2,1)S(1)}, u32[]{:S(2)}, u32[]{:S(2)}) async-start(bf16[64,8,256]{2,0,1:T(8,128)(2,1)} %bitcast.87), calls=%async_computation.1 | async-start | bytes 524288 | tf_op jit(solution)/shard_map/all_to_all | solution.py:70
  16.1 1.7 copy.180
  17.8 7.2 %all-to-all-done.1 = bf16[64,8,256]{2,0,1:T(8,128)(2,1)S(1)} async-done(((bf16[64,8,256]{2,0,1:T(8,128)(2,1)}), bf16[64,8,256]{2,0,1:T(8,128)(2,1)S(1)}, u32[]{:S(2)}, u32[]{:S(2)}) %all-to-all-start.1) | async-done | bytes 262176 | tf_op jit(solution)/shard_map/all_to_all | solution.py:70
  25.0 3.6 %all-to-all-start.2 = ((bf16[64,8,256]{2,0,1:T(8,128)(2,1)}), bf16[64,8,256]{2,0,1:T(8,128)(2,1)S(1)}, u32[]{:S(2)}, u32[]{:S(2)}) async-start(bf16[64,8,256]{2,0,1:T(8,128)(2,1)} %bitcast.86), calls=%async_computation.2 | async-start | bytes 524288 | tf_op jit(solution)/shard_map/all_to_all | solution.py:71
  28.7 0.7 all-gather.5.cloned.1.call-update
  29.4 0.7 reshape.132
  30.1 0.6 reduce-window.6
  31.1 1.7 copy.182
  32.8 4.4 %all-to-all-done.2 = bf16[64,8,256]{2,0,1:T(8,128)(2,1)S(1)} async-done(((bf16[64,8,256]{2,0,1:T(8,128)(2,1)}), bf16[64,8,256]{2,0,1:T(8,128)(2,1)S(1)}, u32[]{:S(2)}, u32[]{:S(2)}) %all-to-all-start.2) | async-done | bytes 262176 | tf_op jit(solution)/shard_map/all_to_all | solution.py:71
  37.2 3.6 %all-to-all-start = ((bf16[64,8,256]{2,0,1:T(8,128)(2,1)}), bf16[64,8,256]{2,0,1:T(8,128)(2,1)S(1)}, u32[]{:S(2)}, u32[]{:S(2)}) async-start(bf16[64,8,256]{2,0,1:T(8,128)(2,1)} %bitcast.88), calls=%async_computation | async-start | bytes 524288 | tf_op jit(solution)/shard_map/all_to_all | solution.py:69
  41.0 5.2 %all-gather.1 = bf16[4,1,2]{2,1,0:T(2,128)(2,1)S(1)} all-gather(bf16[1,1,2]{2,1,0:T(2,128)(2,1)S(1)} %bitcast.114), channel_id=1, replica_groups=mesh['seg'=4,'ep'=8] {'seg'}, dimensions={0}, use_global_device_ids=true | all-gather | bytes 20 | tf_op jit(solution)/shard_map/all_gather | solution.py:14
  47.1 2.3 all-to-all-done
  49.4 0.6 convert_multiply_fusion.1
  50.0 0.6 convolution_convert_fusion.4
  50.6 7.7 %all-gather = bf16[8,128,128]{2,1,0:T(8,128)(2,1)S(1)} all-gather(bf16[2,128,128]{2,1,0:T(8,128)(2,1)S(1)} %convolution_convert_fusion.4), channel_id=2, replica_groups=mesh['seg'=4,'ep'=8] {'seg'}, dimensions={0}, use_global_device_ids=true | all-gather | bytes 327680 | tf_op jit(solution)/shard_map/all_gather | solution.py:14
  58.3 1.0 fusion.5
  59.4 0.4 fusion.8
  59.8 0.3 copy.138
  60.4 19.6 %psum.7 = f32[64]{0:T(128)S(1)} all-reduce(f32[64]{0:T(128)S(1)} %fusion.30), channel_id=1, replica_groups=mesh['seg'=4,'ep'=8] {'ep'}, use_global_device_ids=true, to_apply=%region_10.11 | all-reduce | flops 64 | bytes 512 | tf_op jit(solution)/shard_map/psum | solution.py:118
  80.0 3.5 %convolution_convert_fusion.1 = bf16[64,6144]{1,0:T(8,128)(2,1)} fusion(bf16[256,6144]{1,0:T(8,128)(2,1)} %all-gather.5.cloned.1.call-done, f32[64,1,256]{2,1,0:T(1,128)S(1)} %slice_convert_fusion, f32[256]{0:T(256)S(1)} %dynamic_slice.20, f32[64]{0:T(128)S(1)} %add_rsqrt_fusion), kind=kOutput, calls=%fused_computation.7 | convolution fusion | flops 201768960 | bytes 3998976 | tf_op jit(solution)/shard_map/dot_general | solution.py:122
  84.3 60.6 %reduce-scatter.3.cloned.1.call-done = bf16[8,6144]{1,0:T(8,128)(2,1)} async-done(((bf16[64,6144]{1,0:T(8,128)(2,1)}), bf16[8,6144]{1,0:T(8,128)(2,1)}) %reduce-scatter.3.cloned.1.call-update) | async-done | bytes 98320 | tf_op jit(solution)/shard_map/reduce_scatter | solution.py:127
  144.8 1.2 fusion.3
  146.1 21.9 %all_to_all.71 = bf16[8,8,6144]{2,1,0:T(8,128)(2,1)} all-to-all(bf16[8,8,6144]{2,1,0:T(8,128)(2,1)S(1)} %bitcast.97), channel_id=1, replica_groups=mesh['seg'=4,'ep'=8] {'ep'}, dimensions={0} | all-to-all | bytes 1572864 | tf_op jit(solution)/shard_map/all_to_all | solution.py:138
  168.2 27.4 %all-gather.7.cloned.1.call-done = bf16[256,6144]{1,0:T(8,128)(2,1)} async-done(((bf16[64,6144]{1,0:T(8,128)(2,1)}), bf16[256,6144]{1,0:T(8,128)(2,1)}) %all-gather.7.cloned.1.call-update) | async-done | bytes 3145744 | tf_op jit(solution)/shard_map/all_gather | solution.py:141
  195.6 15.9 %convolution_convert_fusion = bf16[256,6144]{1,0:T(8,128)(2,1)} fusion(bf16[1,576,6144]{2,1,0:T(8,128)(2,1)} %param.21, bf16[256,6144]{1,0:T(8,128)(2,1)} %all-gather.7.cloned.1.call-done, bf16[1,6144,576]{1,2,0:T(8,128)(2,1)} %param.20), kind=kOutput, calls=%fused_computation.3 | convolution fusion | flops 3626188800 | bytes 20447232 | tf_op jit(solution)/shard_map/dot_general | solution.py:58
  211.7 14.6 %all_to_all.72 = bf16[8,64,256]{2,1,0:T(8,128)(2,1)S(1)} all-to-all(bf16[8,64,256]{2,1,0:T(8,128)(2,1)S(1)} %all_to_all.61), channel_id=1, replica_groups=mesh['seg'=4,'ep'=8] {'ep'}, dimensions={0} | all-to-all | bytes 524288 | tf_op jit(solution)/shard_map/all_to_all | solution.py:108
  226.3 23.2 %reduce-scatter.5.cloned.1.call-done = bf16[64,6144]{1,0:T(8,128)(2,1)} async-done(((bf16[256,6144]{1,0:T(8,128)(2,1)}), bf16[64,6144]{1,0:T(8,128)(2,1)}) %reduce-scatter.5.cloned.1.call-update) | async-done | bytes 786448 | tf_op jit(solution)/shard_map/reduce_scatter | solution.py:142
  249.5 5.5 %all-to-all-start.5 = ((bf16[8,8,6144]{2,1,0:T(8,128)(2,1)}), bf16[8,8,6144]{2,1,0:T(8,128)(2,1)S(1)}, u32[]{:S(2)}, u32[]{:S(2)}) async-start(bf16[8,8,6144]{2,1,0:T(8,128)(2,1)} %bitcast.104), calls=%async_computation.7 | async-start | bytes 1572864 | tf_op jit(solution)/shard_map/all_to_all | solution.py:148
  255.4 0.8 multiply_convert_fusion.2
  256.2 18.9 %all-to-all-done.5 = bf16[8,8,6144]{2,1,0:T(8,128)(2,1)S(1)} async-done(((bf16[8,8,6144]{2,1,0:T(8,128)(2,1)}), bf16[8,8,6144]{2,1,0:T(8,128)(2,1)S(1)}, u32[]{:S(2)}, u32[]{:S(2)}) %all-to-all-start.5) | async-done | bytes 786464 | tf_op jit(solution)/shard_map/all_to_all | solution.py:148
  275.2 1.2 convolution_convert_fusion.3
  (51 shorter events, 3.6 us)
Async XLA Ops:
  7.2 39.6 %copy-start = (f32[2048]{0:T(1024)S(1)}, f32[2048]{0:T(1024)}, u32[]{:S(2)}) copy-start(f32[2048]{0:T(1024)} %param.16) | copy-start | bytes 24580
  8.8 16.2 %all-to-all-start.1 = ((bf16[64,8,256]{2,0,1:T(8,128)(2,1)}), bf16[64,8,256]{2,0,1:T(8,128)(2,1)S(1)}, u32[]{:S(2)}, u32[]{:S(2)}) async-start(bf16[64,8,256]{2,0,1:T(8,128)(2,1)} %bitcast.87), calls=%async_computation.1 | async-start | bytes 524288 | tf_op jit(solution)/shard_map/all_to_all | solution.py:70
  25.0 12.2 %all-to-all-start.2 = ((bf16[64,8,256]{2,0,1:T(8,128)(2,1)}), bf16[64,8,256]{2,0,1:T(8,128)(2,1)S(1)}, u32[]{:S(2)}, u32[]{:S(2)}) async-start(bf16[64,8,256]{2,0,1:T(8,128)(2,1)} %bitcast.86), calls=%async_computation.2 | async-start | bytes 524288 | tf_op jit(solution)/shard_map/all_to_all | solution.py:71
  28.6 51.3 %all-gather.5.cloned.1.call-start = ((), (), s32[]{:S(2)}) async-start(), calls=%async_computation.8 | async-start | bytes 3932160 | tf_op jit(solution)/shard_map/all_gather | solution.py:124
  37.2 12.1 %all-to-all-start = ((bf16[64,8,256]{2,0,1:T(8,128)(2,1)}), bf16[64,8,256]{2,0,1:T(8,128)(2,1)S(1)}, u32[]{:S(2)}, u32[]{:S(2)}) async-start(bf16[64,8,256]{2,0,1:T(8,128)(2,1)} %bitcast.88), calls=%async_computation | async-start | bytes 524288 | tf_op jit(solution)/shard_map/all_to_all | solution.py:69
  40.8 104.1 %reduce-scatter.3.cloned.1.call-start = ((), (), s32[]{:S(2)}) async-start(), calls=%async_computation.9 | async-start | bytes 884736 | tf_op jit(solution)/shard_map/reduce_scatter | solution.py:127
  59.8 23.8 %copy-start.1 = (s32[8,2]{0,1:T(2,128)S(1)}, s32[8,2]{0,1:T(2,128)}, u32[]{:S(2)}) copy-start(s32[8,2]{0,1:T(2,128)} %param.18) | copy-start | bytes 196
  83.5 112.1 %all-gather.7.cloned.1.call-start = ((), (), s32[]{:S(2)}) async-start(), calls=%async_computation.10 | async-start | bytes 3932160 | tf_op jit(solution)/shard_map/all_gather | solution.py:141
  168.0 81.5 %reduce-scatter.5.cloned.1.call-start = ((), (), s32[]{:S(2)}) async-start(), calls=%async_computation.11 | async-start | bytes 3932160 | tf_op jit(solution)/shard_map/reduce_scatter | solution.py:142
  211.5 43.6 %copy-start.2 = (f32[8,2]{0,1:T(2,128)S(1)}, f32[8,2]{0,1:T(2,128)}, u32[]{:S(2)}) copy-start(f32[8,2]{0,1:T(2,128)} %param.19) | copy-start | bytes 196
  249.5 25.6 %all-to-all-start.5 = ((bf16[8,8,6144]{2,1,0:T(8,128)(2,1)}), bf16[8,8,6144]{2,1,0:T(8,128)(2,1)S(1)}, u32[]{:S(2)}, u32[]{:S(2)}) async-start(bf16[8,8,6144]{2,1,0:T(8,128)(2,1)} %bitcast.104), calls=%async_computation.7 | async-start | bytes 1572864 | tf_op jit(solution)/shard_map/all_to_all | solution.py:148
Sparse Core Ops, SparseCore 0:
  31.0 31.3 all-gather.4
  83.6 61.1 reduce-scatter.2
  168.1 27.4 all-gather.6
  211.6 37.8 reduce-scatter.4
where the time goes:
time: 284 us; the launch traced here: 283 us
  waiting for transfers between devices  145 us (51%)
  blocking collectives  69 us (24%)
  matrix products  23.7 us (8%)
  starting transfers between devices  20.3 us (7%)
  between operations  14 us (5%)
  local copies, waits for them, and re-layouts  7.68 us (3%)
  other arithmetic  3.54 us (1%)
    reduce_scatter x1, waiting for transfers between devices, on_device(): lax.psum_scatter(proj_terms.astype(jnp.bfloat16), 'ep', scatter_dimension...  60.6 us
    all_gather x1, waiting for transfers between devices, on_device(): gathered = lax.all_gather(arrived, 'seg', axis=0, tiled=True)  27.4 us
    reduce_scatter x1, waiting for transfers between devices, on_device(): lax.psum_scatter(expert_output(gathered, up_piece, down_piece).astype(jnp...  23.2 us
    all_to_all x1, blocking collectives, on_device(): lax.all_to_all(outgoing, 'ep', split_axis=0, concat_axis=0, tiled=True)  21.9 us
    psum x1, blocking collectives, on_device(): square_sums = lax.psum(jnp.sum(picked_float * picked_float, axis=1), 'ep')  19.6 us
    all_to_all x1, waiting for transfers between devices, on_device(): lax.all_to_all(owned_sums.reshape(ep_count, capacity, model_width).astype...  18.9 us
    dot_general x1, matrix products, expert_output(): return jnp.dot(hidden, down_piece, preferred_element_type=jnp.float32)  15.9 us
    all_to_all x1, blocking collectives, on_device(): lax.all_to_all(mixture, 'ep', split_axis=0, concat_axis=1, tiled=True)  14.6 us
  transfers between devices with their start and end apart: 8, of which 7 were waited for; matrix products, arithmetic and copies ran while one was open for 4% of the time, Pallas kernels for 0%

commit v1 on v0

--- a/solution.py
+++ b/solution.py
@@ -1,11 +1,16 @@
+import functools
 import math
 
 import jax
 import jax.numpy as jnp
 from jax import lax
+from jax.experimental import pallas as pl
+from jax.experimental.pallas import tpu as pltpu
 from jax.sharding import PartitionSpec as P
 
 epsilon = 1e-06
+MESH = pl.DeviceIdType.MESH
+VM = pltpu.VMEM
 
 
 def prefix(x, axis, join, neutral):
@@ -58,7 +63,7 @@
     return jnp.dot(hidden, down_piece, preferred_element_type=jnp.float32)
 
 
-def on_device(
+def on_device_routed(
     queries, keys, values, log_decay, out_gain, out_proj, experts, gates, up_weight, down_weight
 ):
     highest = lax.Precision.HIGHEST
@@ -159,6 +164,422 @@
     return (attn_out, moe_out)
 
 
+def remote(src, dst, send, recv, **target):
+    return pltpu.make_async_remote_copy(
+        src_ref=src, dst_ref=dst, send_sem=send, recv_sem=recv,
+        device_id=target, device_id_type=MESH,
+    )
+
+
+def greet(seg_count, ep_count):
+    seg, ep = lax.axis_index("seg"), lax.axis_index("ep")
+    barrier = pltpu.get_barrier_semaphore()
+    for j in range(1, ep_count):
+        pl.semaphore_signal(
+            barrier, inc=1, device_id={"ep": lax.rem(ep + j, ep_count)}, device_id_type=MESH
+        )
+    for k in range(1, seg_count):
+        pl.semaphore_signal(
+            barrier, inc=1, device_id={"seg": lax.rem(seg + k, seg_count)}, device_id_type=MESH
+        )
+    pl.semaphore_wait(barrier, ep_count + seg_count - 2)
+    return seg, ep
+
+
+def mix_kernel(
+    seg_count, ep_count, heads, dim,
+    q_ref, k_ref, v_ref, cum_ref, across_ref, gate_ref,
+    mix_ref, picked_ref, table_ref,
+    qb, kb, vb, states, ends,
+    in_send, in_recv, gate_send, gate_recv, st_send, st_recv, end_send, end_recv, row_send, row_recv,
+):
+    seg, ep = greet(seg_count, ep_count)
+    width = heads * dim
+    triples = ((q_ref, qb), (k_ref, kb), (v_ref, vb))
+    table_ref[seg, ep] = gate_ref[...]
+    sends, gates = [], []
+    for j in range(1, ep_count):
+        other = lax.rem(ep + j, ep_count)
+        columns = pl.ds(pl.multiple_of(other * width, width), width)
+        for i, (ref, buf) in enumerate(triples):
+            copy = remote(
+                ref.at[:, columns], buf.at[ep], in_send.at[i, j], in_recv.at[i, j], ep=other
+            )
+            copy.start()
+            sends.append(copy)
+        copy = remote(
+            gate_ref, table_ref.at[seg, ep], gate_send.at[j], gate_recv.at[j], ep=other
+        )
+        copy.start()
+        gates.append(copy)
+    own = pl.ds(pl.multiple_of(ep * width, width), width)
+    for ref, buf in triples:
+        buf[ep] = ref[:, own]
+    for copy in sends:
+        copy.wait()
+    length = q_ref.shape[0] * ep_count
+    queries, keys, values = (
+        jnp.concatenate([b[p] for p in range(ep_count)], axis=0) for b in (qb, kb, vb)
+    )
+    cum, across = cum_ref[...], across_ref[...]
+    ending = cum[length - 1 : length, :]
+    unit = (
+        lax.broadcasted_iota(jnp.int32, (dim, dim), 0)
+        == lax.broadcasted_iota(jnp.int32, (dim, dim), 1)
+    ).astype(jnp.float32).astype(jnp.bfloat16)
+    for h in range(heads):
+        cols = slice(h * dim, (h + 1) * dim)
+        to_end = jnp.exp(ending[:, h : h + 1] - across[h : h + 1, :])
+        turned = lax.dot_general(
+            unit, keys[:, cols], (((1,), (1,)), ((), ())), preferred_element_type=jnp.float32
+        )
+        states[seg, h] = jnp.dot(
+            (turned * to_end).astype(jnp.bfloat16), values[:, cols],
+            preferred_element_type=jnp.float32,
+        ).astype(jnp.bfloat16)
+        ends[seg, h : h + 1] = jnp.broadcast_to(ending[:, h : h + 1], (1, dim))
+    for copy in gates:
+        copy.wait()
+    moved = []
+    for k in range(1, seg_count):
+        other = lax.rem(seg + k, seg_count)
+        for buf, send, recv in (
+            (states, st_send, st_recv), (ends, end_send, end_recv), (table_ref, row_send, row_recv)
+        ):
+            copy = remote(buf.at[seg], buf.at[seg], send.at[k], recv.at[k], seg=other)
+            copy.start()
+            moved.append(copy)
+    rows = lax.broadcasted_iota(jnp.int32, (length, length), 0)
+    columns = lax.broadcasted_iota(jnp.int32, (length, length), 1)
+    causal = rows >= columns
+    inside = []
+    for h in range(heads):
+        cols = slice(h * dim, (h + 1) * dim)
+        gap = cum[:, h : h + 1] - across[h : h + 1, :]
+        weight = jnp.where(causal, jnp.exp(jnp.where(causal, gap, 0.0)), 0.0)
+        scores = lax.dot_general(
+            queries[:, cols], keys[:, cols], (((1,), (1,)), ((), ())),
+            preferred_element_type=jnp.float32,
+        )
+        inside.append(
+            jnp.dot(
+                (scores * weight).astype(jnp.bfloat16), values[:, cols],
+                preferred_element_type=jnp.float32,
+            )
+        )
+    for copy in moved:
+        copy.wait()
+    outs = []
+    for h in range(heads):
+        cols = slice(h * dim, (h + 1) * dim)
+        carried = jnp.zeros((dim, dim), jnp.float32)
+        for c in range(seg_count):
+            joined = jnp.exp(ends[c, h : h + 1]) * carried + states[c, h].astype(jnp.float32)
+            carried = jnp.where(c < seg, joined, carried)
+        outside = jnp.exp(cum[:, h : h + 1]) * jnp.dot(
+            queries[:, cols], carried.astype(jnp.bfloat16), preferred_element_type=jnp.float32
+        )
+        outs.append((inside[h] + outside).astype(jnp.bfloat16))
+    mixture = jnp.concatenate(outs, axis=1)
+    mix_ref[...] = mixture.reshape(mix_ref.shape)
+    count = picked_ref.shape[0]
+    stride = length // count
+    pick = (
+        lax.broadcasted_iota(jnp.int32, (count, length), 1)
+        == stride * lax.broadcasted_iota(jnp.int32, (count, length), 0)
+    )
+    picked_ref[...] = jnp.dot(
+        pick.astype(jnp.float32).astype(jnp.bfloat16), mixture, preferred_element_type=jnp.float32
+    ).astype(jnp.bfloat16)
+
+
+def expert_kernel(
+    seg_count, ep_count, tile,
+    mix_ref, picked_ref, table_ref, gain_ref, own_gain_ref, proj_hbm, up_hbm, down_hbm,
+    attn_ref, out_ref,
+    up, down, proj, rows, part, sums, full, acc, hidden, tokens,
+    terms, core_in, y_out, y_in, ep_out, ep_in,
+    load_sem, row_send, row_recv, rs_send, rs_recv, ag_send, ag_recv, y_send, y_recv,
+    c_send, c_recv, t_send, t_recv, tc_send, tc_recv, ty_send, ty_recv, te_send, te_recv,
+):
+    f32, bf16 = jnp.float32, jnp.bfloat16
+    seg, ep = greet(seg_count, ep_count)
+    y_count = seg_count // 2
+    core, y = lax.rem(seg, 2), lax.div(seg, 2)
+    mate = seg + 1 - 2 * core
+    own_rows, width = picked_ref.shape
+    total = own_rows * seg_count
+    chunk = total // ep_count
+    cols = proj.shape[1]
+    rows[seg] = picked_ref[...]
+    moved = []
+    for k in range(1, seg_count):
+        copy = remote(
+            picked_ref, rows.at[seg], row_send.at[k], row_recv.at[k],
+            seg=lax.rem(seg + k, seg_count),
+        )
+        copy.start()
+        moved.append(copy)
+    loads = [
+        pltpu.make_async_copy(proj_hbm, proj, load_sem.at[0]),
+        pltpu.make_async_copy(up_hbm.at[0], up, load_sem.at[1]),
+        pltpu.make_async_copy(down_hbm.at[0], down, load_sem.at[2]),
+    ]
+    for load in loads:
+        load.start()
+    for copy in moved:
+        copy.wait()
+    picked = rows[...].reshape(total, width).astype(f32)
+    squares = jnp.sum(picked * picked, axis=1, keepdims=True)
+    high = squares.astype(bf16).astype(f32)
+    lane = lax.broadcasted_iota(jnp.int32, (total, 128), 1)
+    pair = jnp.where(lane < 64, high, squares - high).astype(bf16)
+    part[:, :, cols:] = pair.reshape(ep_count, chunk, 128)
+    scaled = (picked * own_gain_ref[...]).astype(bf16)
+    loads[0].wait()
+    for n in range(0, cols, tile):
+        part[:, :, n : n + tile] = (
+            jnp.dot(scaled, proj[:, n : n + tile], preferred_element_type=f32)
+            .astype(bf16)
+            .reshape(ep_count, chunk, tile)
+        )
+    moved = []
+    for j in range(1, ep_count):
+        other = lax.rem(ep + j, ep_count)
+        copy = remote(part.at[other], sums.at[j], rs_send.at[j], rs_recv.at[j], ep=other)
+        copy.start()
+        moved.append(copy)
+    summed = part[ep].astype(f32)
+    for j, copy in enumerate(moved):
+        copy.wait()
+        summed = summed + sums[j + 1].astype(f32)
+    features = width * ep_count
+    square = summed[:, cols : cols + 1] + summed[:, cols + 64 : cols + 65]
+    inv_rms = lax.rsqrt(square / features + epsilon)
+    full[seg, ep] = (summed[:, :cols] * inv_rms).astype(bf16)
+    gathers = []
+    for j in range(1, ep_count):
+        other = lax.rem(ep + j, ep_count)
+        copy = remote(full.at[seg, ep], full.at[seg, ep], ag_send.at[j], ag_recv.at[j], ep=other)
+        copy.start()
+        gathers.append(copy)
+    y_copies, core_copies = [], []
+    for j in range(ep_count):
+        if j > 0:
+            gathers[j - 1].wait_recv()
+        place = full.at[seg, lax.rem(ep - j + ep_count, ep_count)]
+        for k in range(1, y_count):
+            copy = remote(
+                place, place, y_send.at[j, k], y_recv.at[j, k],
+                seg=lax.rem(y + k, y_count) * 2 + core,
+            )
+            copy.start()
+            y_copies.append((j, k, copy))
+        copy = remote(place, place, c_send.at[j, 0], c_recv.at[j, 0], seg=mate)
+        copy.start()
+        core_copies.append(copy)
+    loads[1].wait()
+    acc[...] = jnp.zeros_like(acc)
+
+    def multiply(s):
+        def step(n, carry):
+            at = pl.multiple_of(n * tile, tile)
+            block = full[s, :, :, pl.ds(at, tile)].reshape(total, tile)
+            lines = pl.ds(pl.multiple_of(s * cols + n * tile, tile), tile)
+            acc[...] += jnp.dot(block, up[lines, :], preferred_element_type=f32)
+            return carry
+
+        lax.fori_loop(0, cols // tile, step, 0)
+
+    multiply(seg)
+    for j, k, copy in y_copies:
+        copy.wait_recv()
+        source = lax.rem(y - k + y_count, y_count) * 2 + core
+        place = full.at[source, lax.rem(ep - j + ep_count, ep_count)]
+        copy = remote(place, place, c_send.at[j, k], c_recv.at[j, k], seg=mate)
+        copy.start()
+        core_copies.append(copy)
+    for k in range(1, y_count):
+        multiply(lax.rem(y - k + y_count, y_count) * 2 + core)
+    for copy in core_copies:
+        copy.wait()
+    for copy in gathers:
+        copy.wait_send()
+    for _, _, copy in y_copies:
+        copy.wait_send()
+    backs = []
+    tokens[ep] = mix_ref[ep]
+    for j in range(1, ep_count):
+        other = lax.rem(ep + j, ep_count)
+        copy = remote(mix_ref.at[other], tokens.at[ep], t_send.at[j], t_recv.at[j], ep=other)
+        copy.start()
+        backs.append(copy)
+    for k in range(y_count):
+        multiply(lax.rem(y + k, y_count) * 2 + 1 - core)
+    value = acc[...]
+    hidden[...] = (value / (1.0 + jnp.exp(-value))).astype(bf16)
+    table = table_ref[...].reshape(total, 128)
+    gate = jnp.sum(jnp.where(lane == lax.div(ep, 2), table, 0.0), axis=1, keepdims=True)
+    loads[2].wait()
+    steps = seg_count
+    core_moves, y_moves, ep_moves = {}, {}, {}
+
+    def product(c):
+        for n in range(0, cols, tile):
+            at = c * cols + n
+            value = jnp.dot(hidden[...], down[:, at : at + tile], preferred_element_type=f32)
+            value = jnp.where(gate != 0.0, value * gate, 0.0).astype(bf16)
+            terms[c, :, :, n : n + tile] = value.reshape(seg_count, own_rows, tile)
+        core_moves[c] = []
+        for k in range(y_count):
+            copy = remote(
+                terms.at[c, k * 2 + 1 - core], core_in.at[c, k],
+                tc_send.at[c, k], tc_recv.at[c, k], seg=mate,
+            )
+            copy.start()
+            core_moves[c].append(copy)
+
+    def across(c):
+        for copy in core_moves[c]:
+            copy.wait()
+        y_moves[c] = []
+        for k in range(1, y_count):
+            other = lax.rem(y + k, y_count)
+            y_out[c, k] = (
+                terms[c, other * 2 + core].astype(f32) + core_in[c, other].astype(f32)
+            ).astype(bf16)
+            copy = remote(
+                y_out.at[c, k], y_in.at[c, k], ty_send.at[c, k], ty_recv.at[c, k],
+                seg=other * 2 + core,
+            )
+            copy.start()
+            y_moves[c].append(copy)
+
+    def along(c):
+        value = terms[c, seg].astype(f32) + core_in[c, y].astype(f32)
+        for k, copy in enumerate(y_moves[c]):
+            copy.wait()
+            value = value + y_in[c, k + 1].astype(f32)
+        ep_out[c] = value.astype(bf16).reshape(ep_count, own_rows // ep_count, cols)
+        ep_moves[c] = []
+        for j in range(1, ep_count):
+            other = lax.rem(ep + j, ep_count)
+            copy = remote(
+                ep_out.at[c, other], ep_in.at[c, j], te_send.at[c, j], te_recv.at[c, j], ep=other
+            )
+            copy.start()
+            ep_moves[c].append(copy)
+
+    for c in range(steps + 2):
+        if c < steps:
+            product(c)
+        if 0 <= c - 1 < steps:
+            across(c - 1)
+        if 0 <= c - 2 < steps:
+            along(c - 2)
+    for copy in backs:
+        copy.wait()
+    mixed = [tokens[p].astype(f32) for p in range(ep_count)]
+    square = sum(jnp.sum(m * m, axis=1, keepdims=True) for m in mixed)
+    inv_rms = lax.rsqrt(square / features + epsilon)
+    for p in range(ep_count):
+        at = slice(p * width, (p + 1) * width)
+        attn_ref[:, at] = (mixed[p] * inv_rms * gain_ref[:, at]).astype(bf16)
+    for c in range(steps):
+        value = ep_out[c, ep].astype(f32)
+        for j, copy in enumerate(ep_moves[c]):
+            copy.wait()
+            value = value + ep_in[c, j + 1].astype(f32)
+        out_ref[:, c * cols : (c + 1) * cols] = value.astype(bf16)
+
+
+def on_device_dense(
+    queries, keys, values, log_decay, out_gain, out_proj, experts, gates, up_weight, down_weight
+):
+    f32, bf16 = jnp.float32, jnp.bfloat16
+    dma = pltpu.SemaphoreType.DMA
+    seg_count, ep_count = lax.axis_size("seg"), lax.axis_size("ep")
+    y_count = seg_count // 2
+    tokens_own, features = queries.shape
+    length, heads = log_decay.shape
+    width = features // ep_count
+    dim = width // heads
+    moe_own = experts.shape[0]
+    seg_rows = moe_own * ep_count
+    total = seg_rows * seg_count
+    cols = out_proj.shape[1]
+    model = up_weight.shape[1]
+    units = up_weight.shape[2]
+    cumulative = jnp.cumsum(log_decay, axis=0)
+    ids = jnp.arange(128, dtype=jnp.int32)[None, None, :]
+    table = jnp.sum(jnp.where(experts[:, :, None] == ids, gates[:, :, None], 0.0), axis=1)
+    vmem = pl.BlockSpec(memory_space=pltpu.VMEM)
+    hbm = pl.BlockSpec(memory_space=pl.ANY)
+    mixture, picked, all_gates = pl.pallas_call(
+        functools.partial(mix_kernel, seg_count, ep_count, heads, dim),
+        out_shape=(
+            jax.ShapeDtypeStruct((ep_count, tokens_own, width), bf16),
+            jax.ShapeDtypeStruct((seg_rows, width), bf16),
+            jax.ShapeDtypeStruct((seg_count, ep_count, moe_own, 128), f32),
+        ),
+        in_specs=[vmem] * 6,
+        out_specs=(vmem,) * 3,
+        scratch_shapes=[VM((ep_count, tokens_own, width), bf16)] * 3
+        + [VM((seg_count, heads, dim, dim), bf16), VM((seg_count, 8, dim), f32)]
+        + [dma((3, ep_count))] * 2
+        + [dma((ep_count,))] * 2
+        + [dma((seg_count,))] * 6,
+        compiler_params=pltpu.CompilerParams(
+            collective_id=1, has_side_effects=True, vmem_limit_bytes=48 * 2**20
+        ),
+    )(queries, keys, values, cumulative, cumulative.T, table)
+    own_gain = lax.dynamic_slice_in_dim(out_gain, lax.axis_index("ep") * width, width, 0)
+    chunk = total // ep_count
+    return pl.pallas_call(
+        functools.partial(expert_kernel, seg_count, ep_count, math.gcd(cols, 512)),
+        out_shape=(
+            jax.ShapeDtypeStruct((tokens_own, features), bf16),
+            jax.ShapeDtypeStruct((moe_own, model), bf16),
+        ),
+        in_specs=[vmem] * 5 + [hbm] * 3,
+        out_specs=(vmem, vmem),
+        scratch_shapes=[
+            VM((model, units), bf16),
+            VM((units, model), bf16),
+            VM((width, cols), bf16),
+            VM((seg_count, seg_rows, width), bf16),
+            VM((ep_count, chunk, cols + 128), bf16),
+            VM((ep_count, chunk, cols + 128), bf16),
+            VM((seg_count, ep_count, chunk, cols), bf16),
+            VM((total, units), f32),
+            VM((total, units), bf16),
+            VM((ep_count, tokens_own, width), bf16),
+            VM((seg_count, seg_count, seg_rows, cols), bf16),
+            VM((seg_count, y_count, seg_rows, cols), bf16),
+            VM((seg_count, y_count, seg_rows, cols), bf16),
+            VM((seg_count, y_count, seg_rows, cols), bf16),
+            VM((seg_count, ep_count, moe_own, cols), bf16),
+            VM((seg_count, ep_count, moe_own, cols), bf16),
+            dma((3,)),
+        ]
+        + [dma((seg_count,))] * 2
+        + [dma((ep_count,))] * 4
+        + [dma((ep_count, y_count))] * 4
+        + [dma((ep_count,))] * 2
+        + [dma((seg_count, y_count))] * 4
+        + [dma((seg_count, ep_count))] * 2,
+        compiler_params=pltpu.CompilerParams(
+            collective_id=2, has_side_effects=True, vmem_limit_bytes=60 * 2**20
+        ),
+    )(mixture, picked, all_gates, out_gain[None, :], own_gain[None, :], out_proj, up_weight, down_weight)
+
+
+def on_device(*args):
+    experts, ep_count = args[6], lax.axis_size("ep")
+    full_rows = max(2, 4 * experts.shape[0] // (ep_count // 2)) >= experts.shape[0]
+    return (on_device_dense if full_rows else on_device_routed)(*args)
+
+
 def solution(mesh):
     placed = (
         P(("seg", "ep"), None),

time: 284 us -> 144 us (0.51)
  waiting for transfers between devices: 145 us -> 0 us
  Pallas kernels: 0 us -> 120 us
  blocking collectives: 69 us -> 0 us
  matrix products: 23.7 us -> 0 us
  starting transfers between devices: 20.3 us -> 0 us
  between operations: 14 us -> 0.68 us
  local copies, waits for them, and re-layouts: 7.68 us -> 20.8 us
    pallas_call x0 -> x2, Pallas kernels: none -> 120 us  [the longest x1 93.9 us: on_device_dense(): pl.pallas_call(functools.partial(expert_kernel, seg_count, ep_count, math...]
    reduce_scatter x2 -> x0, waiting for transfers between devices: 83.8 us -> none  [the longest x1 60.6 us: on_device(): lax.psum_scatter(proj_terms.astype(jnp.bfloat16), 'ep', scatter_dimension...]
    all_to_all x2 -> x0, blocking collectives: 36.5 us -> none  [the longest x1 21.9 us: on_device(): lax.all_to_all(outgoing, 'ep', split_axis=0, concat_axis=0, tiled=True)]
    all_to_all x4 -> x0, waiting for transfers between devices: 32.8 us -> none  [the longest x1 18.9 us: on_device(): lax.all_to_all(owned_sums.reshape(ep_count, capacity, model_width).astype...]
    all_gather x2 -> x0, waiting for transfers between devices: 27.4 us -> none  [the longest x1 27.4 us: on_device(): gathered = lax.all_gather(arrived, 'seg', axis=0, tiled=True)]
    dot_general x7 -> x0, matrix products: 23.7 us -> none  [the longest x1 15.9 us: expert_output(): return jnp.dot(hidden, down_piece, preferred_element_type=jnp.float32)]
    all_to_all x4 -> x0, starting transfers between devices: 20 us -> none  [the longest x1 7.28 us: on_device(): lax.all_to_all(keys, 'ep', split_axis=1, concat_axis=0, tiled=True)]
    psum x1 -> x0, blocking collectives: 19.6 us -> none  [on_device(): square_sums = lax.psum(jnp.sum(picked_float * picked_float, axis=1), 'ep')]
  transfers between devices with their start and end apart: 8 -> 0, of which waited for: 7 -> 0; matrix products, arithmetic and copies ran while one was open for 4% -> 0% of each run, Pallas kernels for 0% -> 0%
where the time goes in v1:
time: 144 us; the launch traced here: 143 us
  Pallas kernels  120 us (83%)
  local copies, waits for them, and re-layouts  20.8 us (14%)
  other arithmetic  1.63 us (1%)
    pallas_call x1, Pallas kernels, on_device_dense(): pl.pallas_call(functools.partial(expert_kernel, seg_count, ep_count, math...  93.9 us
    pallas_call x1, Pallas kernels, on_device_dense(): pl.pallas_call(functools.partial(mix_kernel, seg_count, ep_count, heads,...  26.1 us
    unnamed x16, local copies, waits for them, and re-layouts  18.5 us

profile of v1, /device:TPU:0, one launch (start us, length us, event | category | flops | bytes accessed | tf_op | source)
XLA Modules:
  0.0 143.2 jit_solution(5261374511141058555)
XLA Ops:
  0.6 1.3 dynamic_slice.3
  2.0 0.7 reshape.16
  2.7 0.6 reduce-window.6
  3.3 0.2 slice_reduce_fusion
  3.4 0.2 reduce-window.9
  3.6 0.1 add_bitcast_fusion
  3.7 0.8 select_reduce_fusion.gate_ref
  4.5 0.1 copy.20.cum_ref
  4.6 0.0 copy-start
  4.6 0.9 copy-done
  5.6 0.0 copy-start.1
  5.6 0.9 copy-done.1
  6.5 0.0 copy-start.2
  6.5 0.9 copy-done.2
  7.5 26.1 %shard_map.113 = (bf16[8,64,256]{2,1,0:T(8,128)(2,1)S(1)}, bf16[64,256]{1,0:T(8,128)(2,1)S(1)}, f32[4,8,8,128]{3,2,1,0:T(8,128)S(1)}) custom-call(bf16[64,2048]{1,0:T(8,128)(2,1)S(1)} %copy-done, bf16[64,2048]{1,0:T(8,128)(2,1)S(1)} %copy-done.1, bf16[64,2048]{1,0:T(8,128)(2,1)S(1)} %copy-done.2, f32[512,2]{1,0:T(8,128)S(1)} %copy.20.cum_ref, ...), custom_call_target="tpu_custom_call" | custom-call | tf_op jit(solution)/shard_map/pallas_call | solution.py:518
  33.6 0.0 copy-start.3
  33.6 0.7 copy-done.3
  34.3 0.0 copy-start.4
  34.3 0.6 copy-done.4
  35.0 0.0 copy-start.5
  35.0 0.6 copy-done.5
  35.6 10.5 %copy.21.up_hbm = bf16[1,6144,576]{2,1,0:T(8,128)(2,1)} copy(bf16[1,6144,576]{1,2,0:T(8,128)(2,1)} %param.18) | data formatting | bytes 14155776 | tf_op args[8]
  46.1 93.9 %shard_map.114 = (bf16[64,2048]{1,0:T(8,128)(2,1)}, bf16[8,6144]{1,0:T(8,128)(2,1)}) custom-call(bf16[8,64,256]{2,1,0:T(8,128)(2,1)} %copy-done.3, bf16[64,256]{1,0:T(8,128)(2,1)} %copy-done.5, f32[4,8,8,128]{3,2,1,0:T(8,128)} %copy-done.4, f32[1,2048]{1,0:T(1,128)} %bitcast.15, f32[1,256]{1,0:T(1,128)} %bitcast.18, bf16[256,1536]{1,0:T(8,128)(2,1)} %proj_hbm.1, ...), custom_call_target="tpu_custom_call" | custom-call | tf_op jit(solution)/shard_map/pallas_call | solution.py:538
  140.0 1.7 %copy.29 = bf16[64,2048]{1,0:T(8,128)(2,1)} copy(bf16[64,2048]{1,0:T(8,128)(2,1)} %get-tuple-element.12) | data formatting | bytes 524288
  141.7 1.5 %copy.30 = bf16[8,6144]{1,0:T(8,128)(2,1)} copy(bf16[8,6144]{1,0:T(8,128)(2,1)} %get-tuple-element.13) | data formatting | bytes 196608
  (1 shorter events, 0.0 us)
Async XLA Ops:
  4.6 1.0 copy-start
  5.6 0.9 copy-start.1
  6.5 0.9 copy-start.2
  33.6 0.7 copy-start.3
  34.3 0.6 copy-start.4
  35.0 0.6 copy-start.5

commit v2 on v1

--- a/solution.py
+++ b/solution.py
@@ -186,42 +186,78 @@
     return seg, ep
 
 
-def mix_kernel(
-    seg_count, ep_count, heads, dim,
-    q_ref, k_ref, v_ref, cum_ref, across_ref, gate_ref,
-    mix_ref, picked_ref, table_ref,
-    qb, kb, vb, states, ends,
-    in_send, in_recv, gate_send, gate_recv, st_send, st_recv, end_send, end_recv, row_send, row_recv,
+def step_kernel(
+    seg_count, ep_count, heads, dim, tile,
+    q_ref, k_ref, v_ref, proj_hbm, up_hbm, down_hbm,
+    decay_ref, turned_ref, experts_ref, gates_ref, gain_ref,
+    attn_ref, out_ref,
+    qb, kb, vb, states, ends, table_ref, mix_ref,
+    up, down, proj, rows, part, sums, full, acc, hidden, tokens,
+    terms, core_in, both, y_in, x_in, middle, line, line_in,
+    load_sem, in_send, in_recv, gate_send, gate_recv,
+    st_send, st_recv, end_send, end_recv, row_send, row_recv, pick_send, pick_recv,
+    rs_send, rs_recv, ag_send, ag_recv, x_send, x_recv, y_send, y_recv, c_send, c_recv,
+    t_send, t_recv, tc_send, tc_recv, ty_send, ty_recv, tx_send, tx_recv, tz_send, tz_recv,
 ):
     seg, ep = greet(seg_count, ep_count)
     width = heads * dim
-    triples = ((q_ref, qb), (k_ref, kb), (v_ref, vb))
-    table_ref[seg, ep] = gate_ref[...]
-    sends, gates = [], []
-    for j in range(1, ep_count):
-        other = lax.rem(ep + j, ep_count)
-        columns = pl.ds(pl.multiple_of(other * width, width), width)
-        for i, (ref, buf) in enumerate(triples):
+    tokens_own, moe_own = q_ref.shape[0], experts_ref.shape[0]
+    triples = ((k_ref, kb), (v_ref, vb), (q_ref, qb))
+    sends = {}
+    own = pl.ds(pl.multiple_of(ep * width, width), width)
+    keep = []
+    for i, (ref, buf) in enumerate(triples):
+        sends[i] = []
+        for j in range(1, ep_count):
+            other = lax.rem(ep + j, ep_count)
+            columns = pl.ds(pl.multiple_of(other * width, width), width)
             copy = remote(
                 ref.at[:, columns], buf.at[ep], in_send.at[i, j], in_recv.at[i, j], ep=other
             )
             copy.start()
-            sends.append(copy)
+            sends[i].append(copy)
+        copy = pltpu.make_async_copy(ref.at[:, own], buf.at[ep], load_sem.at[3 + i])
+        copy.start()
+        keep.append(copy)
+    loads = [
+        pltpu.make_async_copy(proj_hbm, proj, load_sem.at[0]),
+        pltpu.make_async_copy(up_hbm.at[0], up, load_sem.at[1]),
+        pltpu.make_async_copy(down_hbm.at[0], down, load_sem.at[2]),
+    ]
+    for load in loads:
+        load.start()
+    lanes = lax.broadcasted_iota(jnp.int32, (moe_own, 128), 1)
+    table_ref[seg, ep] = sum(
+        jnp.where(experts_ref[:, i : i + 1] == lanes, gates_ref[:, i : i + 1], 0.0)
+        for i in range(experts_ref.shape[1])
+    )
+    gates = []
+    for j in range(1, ep_count):
         copy = remote(
-            gate_ref, table_ref.at[seg, ep], gate_send.at[j], gate_recv.at[j], ep=other
+            table_ref.at[seg, ep], table_ref.at[seg, ep], gate_send.at[j], gate_recv.at[j],
+            ep=lax.rem(ep + j, ep_count),
         )
         copy.start()
         gates.append(copy)
-    own = pl.ds(pl.multiple_of(ep * width, width), width)
-    for ref, buf in triples:
-        buf[ep] = ref[:, own]
-    for copy in sends:
+    length = tokens_own * ep_count
+    highest = lax.Precision.HIGHEST
+    rows_at = lax.broadcasted_iota(jnp.int32, (length, length), 0)
+    columns_at = lax.broadcasted_iota(jnp.int32, (length, length), 1)
+    causal = rows_at >= columns_at
+    lower = causal.astype(jnp.float32)
+    cum = jnp.dot(lower, decay_ref[...], precision=highest, preferred_element_type=jnp.float32)
+    across = lax.dot_general(
+        turned_ref[...], lower, (((1,), (1,)), ((), ())), precision=highest,
+        preferred_element_type=jnp.float32,
+    )
+    for copy in keep:
         copy.wait()
-    length = q_ref.shape[0] * ep_count
-    queries, keys, values = (
-        jnp.concatenate([b[p] for p in range(ep_count)], axis=0) for b in (qb, kb, vb)
-    )
-    cum, across = cum_ref[...], across_ref[...]
+    for i in (0, 1):
+        for copy in sends[i]:
+            copy.wait()
+    keys, values = (
+        jnp.concatenate([b[p] for p in range(ep_count)], axis=0) for b in (kb, vb)
+    )
     ending = cum[length - 1 : length, :]
     unit = (
         lax.broadcasted_iota(jnp.int32, (dim, dim), 0)
@@ -249,9 +285,9 @@
             copy = remote(buf.at[seg], buf.at[seg], send.at[k], recv.at[k], seg=other)
             copy.start()
             moved.append(copy)
-    rows = lax.broadcasted_iota(jnp.int32, (length, length), 0)
-    columns = lax.broadcasted_iota(jnp.int32, (length, length), 1)
-    causal = rows >= columns
+    for copy in sends[2]:
+        copy.wait()
+    queries = jnp.concatenate([qb[p] for p in range(ep_count)], axis=0)
     inside = []
     for h in range(heads):
         cols = slice(h * dim, (h + 1) * dim)
@@ -282,51 +318,31 @@
         outs.append((inside[h] + outside).astype(jnp.bfloat16))
     mixture = jnp.concatenate(outs, axis=1)
     mix_ref[...] = mixture.reshape(mix_ref.shape)
-    count = picked_ref.shape[0]
+    count = length // tokens_own * moe_own
     stride = length // count
     pick = (
         lax.broadcasted_iota(jnp.int32, (count, length), 1)
         == stride * lax.broadcasted_iota(jnp.int32, (count, length), 0)
     )
-    picked_ref[...] = jnp.dot(
+    rows[seg] = jnp.dot(
         pick.astype(jnp.float32).astype(jnp.bfloat16), mixture, preferred_element_type=jnp.float32
     ).astype(jnp.bfloat16)
-
-
-def expert_kernel(
-    seg_count, ep_count, tile,
-    mix_ref, picked_ref, table_ref, gain_ref, own_gain_ref, proj_hbm, up_hbm, down_hbm,
-    attn_ref, out_ref,
-    up, down, proj, rows, part, sums, full, acc, hidden, tokens,
-    terms, core_in, y_out, y_in, ep_out, ep_in,
-    load_sem, row_send, row_recv, rs_send, rs_recv, ag_send, ag_recv, y_send, y_recv,
-    c_send, c_recv, t_send, t_recv, tc_send, tc_recv, ty_send, ty_recv, te_send, te_recv,
-):
     f32, bf16 = jnp.float32, jnp.bfloat16
-    seg, ep = greet(seg_count, ep_count)
     y_count = seg_count // 2
     core, y = lax.rem(seg, 2), lax.div(seg, 2)
     mate = seg + 1 - 2 * core
-    own_rows, width = picked_ref.shape
+    own_rows = rows.shape[1]
     total = own_rows * seg_count
     chunk = total // ep_count
     cols = proj.shape[1]
-    rows[seg] = picked_ref[...]
     moved = []
     for k in range(1, seg_count):
         copy = remote(
-            picked_ref, rows.at[seg], row_send.at[k], row_recv.at[k],
+            rows.at[seg], rows.at[seg], pick_send.at[k], pick_recv.at[k],
             seg=lax.rem(seg + k, seg_count),
         )
         copy.start()
         moved.append(copy)
-    loads = [
-        pltpu.make_async_copy(proj_hbm, proj, load_sem.at[0]),
-        pltpu.make_async_copy(up_hbm.at[0], up, load_sem.at[1]),
-        pltpu.make_async_copy(down_hbm.at[0], down, load_sem.at[2]),
-    ]
-    for load in loads:
-        load.start()
     for copy in moved:
         copy.wait()
     picked = rows[...].reshape(total, width).astype(f32)
@@ -335,7 +351,7 @@
     lane = lax.broadcasted_iota(jnp.int32, (total, 128), 1)
     pair = jnp.where(lane < 64, high, squares - high).astype(bf16)
     part[:, :, cols:] = pair.reshape(ep_count, chunk, 128)
-    scaled = (picked * own_gain_ref[...]).astype(bf16)
+    scaled = (picked * gain_ref[:, own]).astype(bf16)
     loads[0].wait()
     for n in range(0, cols, tile):
         part[:, :, n : n + tile] = (
@@ -357,27 +373,54 @@
     square = summed[:, cols : cols + 1] + summed[:, cols + 64 : cols + 65]
     inv_rms = lax.rsqrt(square / features + epsilon)
     full[seg, ep] = (summed[:, :cols] * inv_rms).astype(bf16)
-    gathers = []
-    for j in range(1, ep_count):
-        other = lax.rem(ep + j, ep_count)
-        copy = remote(full.at[seg, ep], full.at[seg, ep], ag_send.at[j], ag_recv.at[j], ep=other)
+    half = ep_count // 2
+    x, z = lax.rem(ep, 2), lax.div(ep, 2)
+    x_mate = ep + 1 - 2 * x
+    flying = []
+
+    def send(place, send_sem, recv_sem, **target):
+        copy = remote(place, place, send_sem, recv_sem, **target)
         copy.start()
-        gathers.append(copy)
-    y_copies, core_copies = [], []
-    for j in range(ep_count):
-        if j > 0:
-            gathers[j - 1].wait_recv()
-        place = full.at[seg, lax.rem(ep - j + ep_count, ep_count)]
-        for k in range(1, y_count):
-            copy = remote(
-                place, place, y_send.at[j, k], y_recv.at[j, k],
-                seg=lax.rem(y + k, y_count) * 2 + core,
-            )
-            copy.start()
-            y_copies.append((j, k, copy))
-        copy = remote(place, place, c_send.at[j, 0], c_recv.at[j, 0], seg=mate)
-        copy.start()
-        core_copies.append(copy)
+        flying.append(copy)
+        return copy
+
+    def on_line(e, k):
+        return lax.rem(e - 2 * k + ep_count, ep_count)
+
+    def y_seg(k):
+        return lax.rem(y + k + y_count, y_count) * 2 + core
+
+    z_copies = {}
+    for k in range(1, half):
+        z_copies[k] = send(
+            full.at[seg, ep], ag_send.at[k], ag_recv.at[k], ep=lax.rem(ep + 2 * k, ep_count)
+        )
+    x_copies, y_copies = {}, {}
+    for k in range(half):
+        if k > 0:
+            z_copies[k].wait_recv()
+        place = full.at[seg, on_line(ep, k)]
+        x_copies[k, 0] = send(place, x_send.at[k, 0], x_recv.at[k, 0], ep=x_mate)
+        for d in range(1, y_count):
+            y_copies[k, 0, d] = send(
+                place, y_send.at[k, 0, d], y_recv.at[k, 0, d], seg=y_seg(d)
+            )
+        send(place, c_send.at[k, 0, 0], c_recv.at[k, 0, 0], seg=mate)
+    for k in range(half):
+        x_copies[k, 0].wait_recv()
+        place = full.at[seg, on_line(x_mate, k)]
+        if k % 2 == 0:
+            for d in range(1, y_count):
+                y_copies[k, 1, d] = send(
+                    place, y_send.at[k, 1, d], y_recv.at[k, 1, d], seg=y_seg(d)
+                )
+        send(place, c_send.at[k, 1, 0], c_recv.at[k, 1, 0], seg=mate)
+        for d in range(1, y_count):
+            y_copies[k, 0, d].wait_recv()
+            place = full.at[y_seg(-d), on_line(ep, k)]
+            if k % 2 == 1:
+                x_copies[k, d] = send(place, x_send.at[k, d], x_recv.at[k, d], ep=x_mate)
+            send(place, c_send.at[k, 0, d], c_recv.at[k, 0, d], seg=mate)
     loads[1].wait()
     acc[...] = jnp.zeros_like(acc)
 
@@ -386,26 +429,29 @@
             at = pl.multiple_of(n * tile, tile)
             block = full[s, :, :, pl.ds(at, tile)].reshape(total, tile)
             lines = pl.ds(pl.multiple_of(s * cols + n * tile, tile), tile)
-            acc[...] += jnp.dot(block, up[lines, :], preferred_element_type=f32)
+            acc[...] += lax.dot_general(
+                block, up[:, lines], (((1,), (1,)), ((), ())), preferred_element_type=f32
+            )
             return carry
 
         lax.fori_loop(0, cols // tile, step, 0)
 
     multiply(seg)
-    for j, k, copy in y_copies:
-        copy.wait_recv()
-        source = lax.rem(y - k + y_count, y_count) * 2 + core
-        place = full.at[source, lax.rem(ep - j + ep_count, ep_count)]
-        copy = remote(place, place, c_send.at[j, k], c_recv.at[j, k], seg=mate)
-        copy.start()
-        core_copies.append(copy)
-    for k in range(1, y_count):
-        multiply(lax.rem(y - k + y_count, y_count) * 2 + core)
-    for copy in core_copies:
-        copy.wait()
-    for copy in gathers:
-        copy.wait_send()
-    for _, _, copy in y_copies:
+    for k in range(half):
+        for d in range(1, y_count):
+            (y_copies[k, 1, d] if k % 2 == 0 else x_copies[k, d]).wait_recv()
+            send(
+                full.at[y_seg(-d), on_line(x_mate, k)],
+                c_send.at[k, 1, d], c_recv.at[k, 1, d], seg=mate,
+            )
+    for d in range(1, y_count):
+        multiply(y_seg(-d))
+    for k in range(half):
+        for i in range(2):
+            for d in range(y_count):
+                place = full.at[seg, ep]
+                remote(place, place, c_send.at[k, i, d], c_recv.at[k, i, d], seg=mate).wait_recv()
+    for copy in flying:
         copy.wait_send()
     backs = []
     tokens[ep] = mix_ref[ep]
@@ -422,7 +468,7 @@
     gate = jnp.sum(jnp.where(lane == lax.div(ep, 2), table, 0.0), axis=1, keepdims=True)
     loads[2].wait()
     steps = seg_count
-    core_moves, y_moves, ep_moves = {}, {}, {}
+    core_moves = {}
 
     def product(c):
         for n in range(0, cols, tile):
@@ -439,44 +485,93 @@
             copy.start()
             core_moves[c].append(copy)
 
-    def across(c):
+    first, second, last = {}, {}, {}
+    mine = own_rows // ep_count
+
+    def joined(c):
         for copy in core_moves[c]:
             copy.wait()
-        y_moves[c] = []
-        for k in range(1, y_count):
-            other = lax.rem(y + k, y_count)
-            y_out[c, k] = (
-                terms[c, other * 2 + core].astype(f32) + core_in[c, other].astype(f32)
+        for k in range(y_count):
+            value = (terms[c, k * 2 + core].astype(f32) + core_in[c, k].astype(f32)).reshape(
+                half, 2, mine, cols
             ).astype(bf16)
+            for i in range(2):
+                both[c, k, i] = value[:, i]
+        first[c] = []
+        if c % 2 == 0:
+            for d in range(1, y_count):
+                first[c].append(
+                    remote(
+                        both.at[c, lax.rem(y + d, y_count)], y_in.at[c, d],
+                        ty_send.at[c, d], ty_recv.at[c, d], seg=y_seg(d),
+                    )
+                )
+        else:
+            first[c].append(
+                remote(
+                    both.at[c, :, 1 - x], x_in.at[c], tx_send.at[c], tx_recv.at[c], ep=x_mate
+                )
+            )
+        for copy in first[c]:
+            copy.start()
+
+    def crossed(c):
+        for copy in first[c]:
+            copy.wait()
+        second[c] = []
+        if c % 2 == 0:
+            for i in range(2):
+                value = both[c, y, i].astype(f32)
+                for d in range(1, y_count):
+                    value = value + y_in[c, d, i].astype(f32)
+                middle[c, i] = value.astype(bf16)
+            second[c].append(
+                remote(
+                    middle.at[c, 1 - x], x_in.at[c, 0], tx_send.at[c], tx_recv.at[c], ep=x_mate
+                )
+            )
+        else:
+            for k in range(y_count):
+                middle[c, k] = (both[c, k, x].astype(f32) + x_in[c, k].astype(f32)).astype(bf16)
+            for d in range(1, y_count):
+                second[c].append(
+                    remote(
+                        middle.at[c, lax.rem(y + d, y_count)], y_in.at[c, d, 0],
+                        ty_send.at[c, d], ty_recv.at[c, d], seg=y_seg(d),
+                    )
+                )
+        for copy in second[c]:
+            copy.start()
+
+    def along(c):
+        for copy in second[c]:
+            copy.wait()
+        if c % 2 == 0:
+            value = middle[c, x].astype(f32) + x_in[c, 0].astype(f32)
+        else:
+            value = middle[c, y].astype(f32)
+            for d in range(1, y_count):
+                value = value + y_in[c, d, 0].astype(f32)
+        line[c] = value.astype(bf16)
+        last[c] = []
+        for k in range(1, half):
+            other = lax.rem(z + k, half)
             copy = remote(
-                y_out.at[c, k], y_in.at[c, k], ty_send.at[c, k], ty_recv.at[c, k],
-                seg=other * 2 + core,
+                line.at[c, other], line_in.at[c, k], tz_send.at[c, k], tz_recv.at[c, k],
+                ep=other * 2 + x,
             )
             copy.start()
-            y_moves[c].append(copy)
-
-    def along(c):
-        value = terms[c, seg].astype(f32) + core_in[c, y].astype(f32)
-        for k, copy in enumerate(y_moves[c]):
-            copy.wait()
-            value = value + y_in[c, k + 1].astype(f32)
-        ep_out[c] = value.astype(bf16).reshape(ep_count, own_rows // ep_count, cols)
-        ep_moves[c] = []
-        for j in range(1, ep_count):
-            other = lax.rem(ep + j, ep_count)
-            copy = remote(
-                ep_out.at[c, other], ep_in.at[c, j], te_send.at[c, j], te_recv.at[c, j], ep=other
-            )
-            copy.start()
-            ep_moves[c].append(copy)
-
-    for c in range(steps + 2):
+            last[c].append(copy)
+
+    for c in range(steps + 3):
         if c < steps:
             product(c)
         if 0 <= c - 1 < steps:
-            across(c - 1)
+            joined(c - 1)
         if 0 <= c - 2 < steps:
-            along(c - 2)
+            crossed(c - 2)
+        if 0 <= c - 3 < steps:
+            along(c - 3)
     for copy in backs:
         copy.wait()
     mixed = [tokens[p].astype(f32) for p in range(ep_count)]
@@ -486,10 +581,10 @@
         at = slice(p * width, (p + 1) * width)
         attn_ref[:, at] = (mixed[p] * inv_rms * gain_ref[:, at]).astype(bf16)
     for c in range(steps):
-        value = ep_out[c, ep].astype(f32)
-        for j, copy in enumerate(ep_moves[c]):
+        value = line[c, z].astype(f32)
+        for j, copy in enumerate(last[c]):
             copy.wait()
-            value = value + ep_in[c, j + 1].astype(f32)
+            value = value + line_in[c, j + 1].astype(f32)
         out_ref[:, c * cols : (c + 1) * cols] = value.astype(bf16)
 
 
@@ -499,52 +594,34 @@
     f32, bf16 = jnp.float32, jnp.bfloat16
     dma = pltpu.SemaphoreType.DMA
     seg_count, ep_count = lax.axis_size("seg"), lax.axis_size("ep")
-    y_count = seg_count // 2
+    y_count, half = seg_count // 2, ep_count // 2
     tokens_own, features = queries.shape
-    length, heads = log_decay.shape
+    heads = log_decay.shape[1]
     width = features // ep_count
     dim = width // heads
     moe_own = experts.shape[0]
     seg_rows = moe_own * ep_count
     total = seg_rows * seg_count
     cols = out_proj.shape[1]
-    model = up_weight.shape[1]
-    units = up_weight.shape[2]
-    cumulative = jnp.cumsum(log_decay, axis=0)
-    ids = jnp.arange(128, dtype=jnp.int32)[None, None, :]
-    table = jnp.sum(jnp.where(experts[:, :, None] == ids, gates[:, :, None], 0.0), axis=1)
+    model, units = up_weight.shape[1:]
+    chunk = total // ep_count
     vmem = pl.BlockSpec(memory_space=pltpu.VMEM)
     hbm = pl.BlockSpec(memory_space=pl.ANY)
-    mixture, picked, all_gates = pl.pallas_call(
-        functools.partial(mix_kernel, seg_count, ep_count, heads, dim),
-        out_shape=(
-            jax.ShapeDtypeStruct((ep_count, tokens_own, width), bf16),
-            jax.ShapeDtypeStruct((seg_rows, width), bf16),
-            jax.ShapeDtypeStruct((seg_count, ep_count, moe_own, 128), f32),
-        ),
-        in_specs=[vmem] * 6,
-        out_specs=(vmem,) * 3,
-        scratch_shapes=[VM((ep_count, tokens_own, width), bf16)] * 3
-        + [VM((seg_count, heads, dim, dim), bf16), VM((seg_count, 8, dim), f32)]
-        + [dma((3, ep_count))] * 2
-        + [dma((ep_count,))] * 2
-        + [dma((seg_count,))] * 6,
-        compiler_params=pltpu.CompilerParams(
-            collective_id=1, has_side_effects=True, vmem_limit_bytes=48 * 2**20
-        ),
-    )(queries, keys, values, cumulative, cumulative.T, table)
-    own_gain = lax.dynamic_slice_in_dim(out_gain, lax.axis_index("ep") * width, width, 0)
-    chunk = total // ep_count
     return pl.pallas_call(
-        functools.partial(expert_kernel, seg_count, ep_count, math.gcd(cols, 512)),
+        functools.partial(step_kernel, seg_count, ep_count, heads, dim, math.gcd(cols, 512)),
         out_shape=(
             jax.ShapeDtypeStruct((tokens_own, features), bf16),
             jax.ShapeDtypeStruct((moe_own, model), bf16),
         ),
-        in_specs=[vmem] * 5 + [hbm] * 3,
+        in_specs=[hbm] * 6 + [vmem] * 5,
         out_specs=(vmem, vmem),
-        scratch_shapes=[
-            VM((model, units), bf16),
+        scratch_shapes=[VM((ep_count, tokens_own, width), bf16)] * 3
+        + [
+            VM((seg_count, heads, dim, dim), bf16),
+            VM((seg_count, 8, dim), f32),
+            VM((seg_count, ep_count, moe_own, 128), f32),
+            VM((ep_count, tokens_own, width), bf16),
+            VM((units, model), bf16),
             VM((units, model), bf16),
             VM((width, cols), bf16),
             VM((seg_count, seg_rows, width), bf16),
@@ -556,22 +633,32 @@
             VM((ep_count, tokens_own, width), bf16),
             VM((seg_count, seg_count, seg_rows, cols), bf16),
             VM((seg_count, y_count, seg_rows, cols), bf16),
-            VM((seg_count, y_count, seg_rows, cols), bf16),
-            VM((seg_count, y_count, seg_rows, cols), bf16),
-            VM((seg_count, ep_count, moe_own, cols), bf16),
-            VM((seg_count, ep_count, moe_own, cols), bf16),
-            dma((3,)),
+            VM((seg_count, y_count, 2, half, moe_own, cols), bf16),
+            VM((seg_count, y_count, 2, half, moe_own, cols), bf16),
+            VM((seg_count, y_count, half, moe_own, cols), bf16),
+            VM((seg_count, max(2, y_count), half, moe_own, cols), bf16),
+            VM((seg_count, half, moe_own, cols), bf16),
+            VM((seg_count, half, moe_own, cols), bf16),
+            dma((6,)),
         ]
-        + [dma((seg_count,))] * 2
-        + [dma((ep_count,))] * 4
-        + [dma((ep_count, y_count))] * 4
+        + [dma((3, ep_count))] * 2
+        + [dma((ep_count,))] * 2
+        + [dma((seg_count,))] * 8
+        + [dma((ep_count,))] * 2
+        + [dma((half,))] * 2
+        + [dma((half, y_count))] * 2
+        + [dma((half, 2, y_count))] * 4
         + [dma((ep_count,))] * 2
         + [dma((seg_count, y_count))] * 4
-        + [dma((seg_count, ep_count))] * 2,
+        + [dma((seg_count,))] * 2
+        + [dma((seg_count, half))] * 2,
         compiler_params=pltpu.CompilerParams(
-            collective_id=2, has_side_effects=True, vmem_limit_bytes=60 * 2**20
+            collective_id=1, has_side_effects=True, vmem_limit_bytes=62 * 2**20
         ),
-    )(mixture, picked, all_gates, out_gain[None, :], own_gain[None, :], out_proj, up_weight, down_weight)
+    )(
+        queries, keys, values, out_proj, jnp.swapaxes(up_weight, 1, 2), down_weight,
+        log_decay, log_decay.T, experts, gates, out_gain[None, :],
+    )
 
 
 def on_device(*args):

time: 144 us -> 119 us (0.83)
  local copies, waits for them, and re-layouts: 20.8 us -> 7.44 us
  Pallas kernels: 120 us -> 111 us
  other arithmetic: 1.63 us -> 0 us
    unnamed x16 -> x5, local copies, waits for them, and re-layouts: 18.5 us -> 7.44 us
    pallas_call x2 -> x1, Pallas kernels: 120 us -> 111 us  [on_device_dense(): pl.pallas_call(functools.partial(step_kernel, seg_count, ep_count, heads,...]
where the time goes in v2:
time: 119 us
  Pallas kernels  111 us (93%)
  local copies, waits for them, and re-layouts  7.44 us (6%)
    pallas_call x1, Pallas kernels, on_device_dense(): pl.pallas_call(functools.partial(step_kernel, seg_count, ep_count, heads,...  111 us
    unnamed x5, local copies, waits for them, and re-layouts  7.44 us

profile of v2, /device:TPU:0, one launch (start us, length us, event | category | flops | bytes accessed | tf_op | source)
XLA Modules:
  0.0 118.9 jit_solution(17902622090524277791)
XLA Ops:
  0.6 1.3 %copy.13.experts_ref = s32[8,2]{1,0:T(8,128)} copy(s32[8,2]{0,1:T(2,128)} %param.16) | data formatting | bytes 128 | tf_op args[6]
  2.0 1.3 %copy.14.gates_ref = f32[8,2]{1,0:T(8,128)} copy(f32[8,2]{0,1:T(2,128)} %param.17) | data formatting | bytes 128 | tf_op args[7]
  3.3 1.5 %copy.12.decay_ref = f32[512,2]{1,0:T(8,128)} copy(f32[512,2]{0,1:T(2,128)} %param.13) | data formatting | bytes 8192 | tf_op args[3]
  4.9 110.8 %shard_map.113 = (bf16[64,2048]{1,0:T(8,128)(2,1)}, bf16[8,6144]{1,0:T(8,128)(2,1)}) custom-call(bf16[64,2048]{1,0:T(8,128)(2,1)} %q_ref.1, bf16[64,2048]{1,0:T(8,128)(2,1)} %k_ref.1, bf16[64,2048]{1,0:T(8,128)(2,1)} %v_ref.1, bf16[256,1536]{1,0:T(8,128)(2,1)} %proj_hbm.1, bf16[1,576,6144]{2,1,0:T(8,128)(2,1)} %bitcast.3, bf16[1,576,6144]{2,1,0:T(8,128)(2,1)} %down_hbm.1, ...), custom_call_target="tpu_custom_call" | custom-call | tf_op jit(solution)/shard_map/pallas_call | solution.py:610
  115.6 1.7 %copy.17 = bf16[64,2048]{1,0:T(8,128)(2,1)} copy(bf16[64,2048]{1,0:T(8,128)(2,1)} %get-tuple-element.4) | data formatting | bytes 524288
  117.3 1.5 %copy.18 = bf16[8,6144]{1,0:T(8,128)(2,1)} copy(bf16[8,6144]{1,0:T(8,128)(2,1)} %get-tuple-element.5) | data formatting | bytes 196608
